TPU v7x, 512 devices: a whole 4x4x16 slice. The times are simulated.
512 devices in a mesh: obj: 16 (over x, z_hi, core), tile: 32 (over y, z_lo).
Axes of the slice: x: 4, y: 4, z: 16 (z_hi: 2, z_lo: 8; z = z_hi * 8 + z_lo), core: 2. Of those that a mesh axis runs over, the one named last changes fastest.
Arguments:
- checkpoints: bfloat16 [6, 12, 48, 32, 128], P(None, None, 'obj', 'tile'), may hold values from 0.19921875 to 2
- courant: float32 [2, 48, 32, 128], P(None, None, 'tile'), may hold values from -0.6 to 0.6
- insolation: float32 [32, 128], P('tile'), may hold values from 0.3 to 3
- region_mask: int32 [16, 32, 128], P('obj', 'tile'), may hold values 0 or 1
- measure_step: int32 [16], P('obj'), may hold values from 1 to 6
- snr_weight: float32 [12, 48], replicated, may hold values from 0.3 to 3
- diffusion_number: float32 [12, 47], replicated, may hold values from 0.1 to 2
- coupling: float32 [12, 12], replicated, may hold values from -1.75 to 1.75
- recombination: float32 [12], replicated, may hold values from 0.05 to 0.25
Outputs:
- state_adjoint: float32 [16, 12, 48, 32, 128], P('obj', None, None, 'tile')
- driver_grad: float32 [16, 6, 12, 48], P('obj')
All inputs are finite; a program needn't handle non-finite values. No bound on the sum of `region_mask` on one device may be relied on, other than what follows from the above.
Results may differ from a plain program's by a relative error of at most 0.0003.
Values may be sent and summed in bfloat16 or wider, within the bound.
A program may use at most 64 MiB of HBM per device.

v0:
```python
import jax
import jax.numpy as jnp
from jax import lax
from jax.sharding import PartitionSpec as P

smoothing = 0.2


def padded_2(block, sides, width):
    for axis, dim in sides:
        count = lax.axis_size(axis)
        forward = [(i, i + 1) for i in range(count - 1)]
        forward.append((count - 1, 0))
        backward = [(target, source) for source, target in forward]
        low = lax.ppermute(
            lax.slice_in_dim(block, block.shape[dim] - width, None, axis=dim), axis, forward
        )
        high = lax.ppermute(lax.slice_in_dim(block, 0, width, axis=dim), axis, backward)
        block = jnp.concatenate([low, block, high], axis=dim)
    return block


def advect_back(adjoint, padded, flux, northward):
    lat_pad = jnp.pad(adjoint, ((0, 0), (0, 0), (0, 0), (1, 1)))
    north_flux = jnp.pad(northward[None] * adjoint, ((0, 0), (0, 0), (0, 0), (1, 1)))
    beside_all = padded[:, :, 2:] + padded[:, :, :-2] + lat_pad[..., 2:] + lat_pad[..., :-2]
    carried = flux[:, :, 2:] - flux[:, :, :-2] + north_flux[..., 2:] - north_flux[..., :-2]
    return (1.0 - 4.0 * smoothing) * adjoint + smoothing * beside_all + 0.5 * carried


def react_back(solved, state, coupling, recombination):
    mixing = jnp.einsum("fg,...flxy->...glxy", coupling, solved, precision=lax.Precision.HIGHEST)
    return (
        solved
        + mixing
        - 2.0 * recombination[:, None, None, None] * state.astype(jnp.float32) * solved
    )


def per_device(
    checkpoints,
    courant,
    insolation,
    region_mask,
    measure_step,
    snr_weight,
    diffusion_number,
    coupling,
    recombination,
):
    steps = checkpoints.shape[0]
    fields, levels = snr_weight.shape
    width, latitudes = insolation.shape
    columns = width * latitudes
    cells = columns * lax.axis_size("tile")
    impulse = region_mask[0].astype(jnp.float32)[None, None] * snr_weight[:, :, None, None]
    below = jnp.pad(diffusion_number, ((0, 0), (1, 0)))
    above = jnp.pad(diffusion_number, ((0, 0), (0, 1)))
    middle = 1.0 + below + above
    eastward = courant[0]
    northward = courant[1]
    adjoint = jnp.zeros((fields, levels, width, latitudes), jnp.float32)
    partials = [None] * steps
    for back in range(steps):
        moment = steps - 1 - back
        arrive = (measure_step[0] == moment + 1).astype(jnp.float32)
        adjoint = adjoint + arrive * impulse
        stacked = jnp.stack([adjoint, eastward[None] * adjoint])
        extended = padded_2(stacked, (("tile", 3),), 1)
        padded = extended[0]
        flux = extended[1]
        advected = advect_back(adjoint, padded, flux, northward)
        solved = lax.linalg.tridiagonal_solve(
            -below, middle, -above, advected.reshape(fields, levels, columns)
        )
        solved = solved.reshape(fields, levels, width, latitudes)
        partial_sum = jnp.einsum("flxy,xy->fl", solved, insolation, precision=lax.Precision.HIGHEST)
        partial_sum = lax.psum(partial_sum, "tile")
        partials[moment] = partial_sum
        state = checkpoints[moment]
        adjoint = react_back(
            solved, lax.all_gather(state, "obj", axis=1, tiled=True), coupling, recombination
        )
    gradients = jnp.stack(partials)
    return (adjoint[None], (gradients / cells)[None])


def solution(mesh):
    return jax.shard_map(
        per_device,
        mesh=mesh,
        in_specs=(
            P(None, None, "obj", "tile", None),
            P(None, None, "tile", None),
            P("tile", None),
            P("obj", "tile", None),
            P("obj"),
            P(),
            P(),
            P(),
            P(),
        ),
        out_specs=(P("obj", None, None, "tile", None), P("obj", None, None, None)),
        check_vma=False,
    )
```

profile of v0, /device:TPU:2, one launch (start us, length us, event | category | flops | bytes accessed | tf_op | source)
XLA Modules:
  0.0 679.5 jit_solution(14576754906486607328)
XLA Ops:
  1.4 0.7 convert_bitcast_fusion
  2.0 0.8 copy.28
  2.8 0.8 fusion.1314
  4.0 15.6 %collective-permute-start.1 = (f32[2,12,48,1,128]{4,2,3,1,0:T(8,128)S(1)}, f32[2,12,48,1,128]{4,2,3,1,0:T(8,128)S(1)}, u32[]{:S(2)}, u32[]{:S(2)}) collective-permute-start(f32[2,12,48,1,128]{4,2,3,1,0:T(8,128)S(1)} %copy.30), channel_id=1, source_target_pairs={{1,0},{2,1},{3,2},{4,3},{5,4},{6,5},{7,6},{8,7},{9,8},{10,9},{11,1... | collective-permute-start | bytes 1769480 | tf_op jit(solution)/shard_map/ppermute | solution.py:18
  19.6 1.9 collective-permute-start
  22.8 53.9 %all-gather = bf16[1,12,48,1,128]{4,1,3,0,2:T(8,128)(2,1)S(1)} all-gather(bf16[1,12,3,1,128]{4,1,3,0,2:T(8,128)(2,1)S(1)} %copy.99), channel_id=2, replica_groups=mesh['obj'=16,'tile'=32] {'obj'}, dimensions={2}, use_global_device_ids=true | all-gather | bytes 156672 | tf_op jit(solution)/shard_map/all_gather | solution.py:82
  77.8 0.5 fusion.29
  78.3 0.5 fusion.1138
  81.5 0.6 fusion.13
  82.4 3.4 collective-permute-start.3
  85.8 2.5 collective-permute-start.2
  88.3 57.2 %all-gather.1 = bf16[1,12,48,1,128]{4,1,3,0,2:T(8,128)(2,1)S(1)} all-gather(bf16[1,12,3,1,128]{4,1,3,0,2:T(8,128)(2,1)S(1)} %copy.100), channel_id=3, replica_groups=mesh['obj'=16,'tile'=32] {'obj'}, dimensions={2}, use_global_device_ids=true | all-gather | bytes 156672 | tf_op jit(solution)/shard_map/all_gather | solution.py:82
  146.9 0.5 fusion.959
  150.1 0.6 fusion.15
  151.0 4.8 collective-permute-start.5
  155.8 1.9 collective-permute-start.4
  157.7 57.7 %all-gather.2 = bf16[1,12,48,1,128]{4,1,3,0,2:T(8,128)(2,1)S(1)} all-gather(bf16[1,12,3,1,128]{4,1,3,0,2:T(8,128)(2,1)S(1)} %copy.101), channel_id=4, replica_groups=mesh['obj'=16,'tile'=32] {'obj'}, dimensions={2}, use_global_device_ids=true | all-gather | bytes 156672 | tf_op jit(solution)/shard_map/all_gather | solution.py:82
  216.4 0.5 fusion.47
  217.0 0.5 fusion.786
  220.1 0.6 fusion.17
  221.0 5.3 collective-permute-start.7
  226.3 1.9 collective-permute-start.6
  228.3 58.2 %all-gather.5 = bf16[1,12,48,1,128]{4,1,3,0,2:T(8,128)(2,1)S(1)} all-gather(bf16[1,12,3,1,128]{4,1,3,0,2:T(8,128)(2,1)S(1)} %copy.104), channel_id=7, replica_groups=mesh['obj'=16,'tile'=32] {'obj'}, dimensions={2}, use_global_device_ids=true | all-gather | bytes 156672 | tf_op jit(solution)/shard_map/all_gather | solution.py:82
  286.5 34.6 %all-gather.3 = bf16[1,12,48,1,128]{4,1,3,0,2:T(8,128)(2,1)S(1)} all-gather(bf16[1,12,3,1,128]{4,1,3,0,2:T(8,128)(2,1)S(1)} %copy.102), channel_id=5, replica_groups=mesh['obj'=16,'tile'=32] {'obj'}, dimensions={2}, use_global_device_ids=true | all-gather | bytes 156672 | tf_op jit(solution)/shard_map/all_gather | solution.py:82
  321.0 45.1 %all-gather.4 = bf16[1,12,48,1,128]{4,1,3,0,2:T(8,128)(2,1)S(1)} all-gather(bf16[1,12,3,1,128]{4,1,3,0,2:T(8,128)(2,1)S(1)} %copy.103), channel_id=6, replica_groups=mesh['obj'=16,'tile'=32] {'obj'}, dimensions={2}, use_global_device_ids=true | all-gather | bytes 156672 | tf_op jit(solution)/shard_map/all_gather | solution.py:82
  366.1 0.9 fusion.84
  368.6 0.5 fusion.613
  371.8 0.6 fusion.19
  372.7 7.7 %collective-permute-start.9 = (f32[2,12,48,1,128]{4,2,3,1,0:T(8,128)S(1)}, f32[2,12,48,1,128]{4,2,3,1,0:T(8,128)S(1)}, u32[]{:S(2)}, u32[]{:S(2)}) collective-permute-start(f32[2,12,48,1,128]{4,2,3,1,0:T(8,128)S(1)} %copy.60), channel_id=1, source_target_pairs={{1,0},{2,1},{3,2},{4,3},{5,4},{6,5},{7,6},{8,7},{9,8},{10,9},{11,1... | collective-permute-start | bytes 1769480 | tf_op jit(solution)/shard_map/ppermute | solution.py:18
  380.4 2.1 collective-permute-start.8
  382.6 0.9 fusion.86
  383.6 0.9 fusion.88
  384.6 9.5 %collective-permute-done.9 = f32[2,12,48,1,128]{4,2,3,1,0:T(8,128)S(1)} collective-permute-done((f32[2,12,48,1,128]{4,2,3,1,0:T(8,128)S(1)}, f32[2,12,48,1,128]{4,2,3,1,0:T(8,128)S(1)}, u32[]{:S(2)}, u32[]{:S(2)}) %collective-permute-start.9) | collective-permute-done | bytes 589856 | tf_op jit(solution)/shard_map/ppermute | solution.py:18
  394.3 12.6 %collective-permute-done.8 = f32[2,12,48,1,128]{4,2,3,1,0:T(8,128)S(1)} collective-permute-done((f32[2,12,48,1,128]{4,2,3,1,0:T(8,128)S(1)}, f32[2,12,48,1,128]{4,2,3,1,0:T(8,128)S(1)}, u32[]{:S(2)}, u32[]{:S(2)}) %collective-permute-start.8) | collective-permute-done | bytes 589856 | tf_op jit(solution)/shard_map/ppermute | solution.py:15
  408.1 0.5 fusion.440
  411.3 0.6 fusion.21
  412.2 5.6 collective-permute-start.11
  417.8 1.9 collective-permute-start.10
  419.7 0.9 fusion.90
  420.8 0.9 fusion.92
  421.7 19.9 %collective-permute-done.11 = f32[2,12,48,1,128]{4,2,3,1,0:T(8,128)S(1)} collective-permute-done((f32[2,12,48,1,128]{4,2,3,1,0:T(8,128)S(1)}, f32[2,12,48,1,128]{4,2,3,1,0:T(8,128)S(1)}, u32[]{:S(2)}, u32[]{:S(2)}) %collective-permute-start.11) | collective-permute-done | bytes 589856 | tf_op jit(solution)/shard_map/ppermute | solution.py:18
  441.9 1.7 collective-permute-done.10
  444.8 0.5 fusion.267
  448.0 0.5 fusion.23
  448.5 1.0 copy.74
  449.6 0.9 fusion.94
  450.5 228.3 %all-reduce.14 = (f32[1,1,12,48]{3,0,2,1:T(1,128)S(1)}, f32[1,1,12,48]{3,0,2,1:T(1,128)S(1)}, f32[1,1,12,48]{3,0,2,1:T(1,128)S(1)}, f32[1,1,12,48]{3,0,2,1:T(1,1...) all-reduce(f32[1,1,12,48]{3,0,2,1:T(1,128)S(1)} %stack.87, ...), channel_id=1, replica_groups=mesh['obj'=16,'tile'=32] {'tile'}, use_global_device_ids=true, to_apply=%region_0.1 | all-reduce | flops 3456 | bytes 27648 | tf_op jit(solution)/shard_map/psum | solution.py:78
  678.9 0.7 broadcast_multiply_fusion.7
  (398 shorter events, 26.8 us)
Async XLA Ops:
  0.6 80.8 %copy-start = (f32[12,12]{1,0:T(8,128)S(1)}, f32[12,12]{1,0:T(8,128)}, u32[]{:S(2)}) copy-start(f32[12,12]{1,0:T(8,128)} %param.16) | copy-start | bytes 1732
  0.6 20.9 %copy-start.3 = (f32[12,47]{1,0:T(8,128)S(1)}, f32[12,47]{1,0:T(8,128)}, u32[]{:S(2)}) copy-start(f32[12,47]{1,0:T(8,128)} %param.15) | copy-start | bytes 6772
  0.7 21.1 %copy-start.1 = (bf16[6,12,3,1,128]{4,2,3,1,0:T(4,128)(2,1)S(1)}, bf16[6,12,3,1,128]{4,2,3,1,0:T(4,128)(2,1)}, u32[]{:S(2)}) copy-start(bf16[6,12,3,1,128]{4,2,3,1,0:T(4,128)(2,1)} %param.9) | copy-start | bytes 165892
  0.7 22.1 %copy-start.4 = (f32[12]{0:T(128)S(1)}, f32[12]{0:T(128)}, u32[]{:S(2)}) copy-start(f32[12]{0:T(128)} %param.17) | copy-start | bytes 148
  4.0 72.9 %collective-permute-start.1 = (f32[2,12,48,1,128]{4,2,3,1,0:T(8,128)S(1)}, f32[2,12,48,1,128]{4,2,3,1,0:T(8,128)S(1)}, u32[]{:S(2)}, u32[]{:S(2)}) collective-permute-start(f32[2,12,48,1,128]{4,2,3,1,0:T(8,128)S(1)} %copy.30), channel_id=1, source_target_pairs={{1,0},{2,1},{3,2},{4,3},{5,4},{6,5},{7,6},{8,7},{9,8},{10,9},{11,1... | collective-permute-start | bytes 1769480 | tf_op jit(solution)/shard_map/ppermute | solution.py:18
  19.6 57.5 %collective-permute-start = (f32[2,12,48,1,128]{4,2,3,1,0:T(8,128)S(1)}, f32[2,12,48,1,128]{4,2,3,1,0:T(8,128)S(1)}, u32[]{:S(2)}, u32[]{:S(2)}) collective-permute-start(f32[2,12,48,1,128]{4,2,3,1,0:T(8,128)S(1)} %copy.30), channel_id=1, source_target_pairs={{0,1},{1,2},{2,3},{3,4},{4,5},{5,6},{6,7},{7,8},{8,9},{9,10},{10,1... | collective-permute-start | bytes 1769480 | tf_op jit(solution)/shard_map/ppermute | solution.py:15
  82.4 63.0 %collective-permute-start.3 = (f32[2,12,48,1,128]{4,2,3,1,0:T(8,128)S(1)}, f32[2,12,48,1,128]{4,2,3,1,0:T(8,128)S(1)}, u32[]{:S(2)}, u32[]{:S(2)}) collective-permute-start(f32[2,12,48,1,128]{4,2,3,1,0:T(8,128)S(1)} %copy.39), channel_id=1, source_target_pairs={{1,0},{2,1},{3,2},{4,3},{5,4},{6,5},{7,6},{8,7},{9,8},{10,9},{11,1... | collective-permute-start | bytes 1769480 | tf_op jit(solution)/shard_map/ppermute | solution.py:18
  85.8 59.8 %collective-permute-start.2 = (f32[2,12,48,1,128]{4,2,3,1,0:T(8,128)S(1)}, f32[2,12,48,1,128]{4,2,3,1,0:T(8,128)S(1)}, u32[]{:S(2)}, u32[]{:S(2)}) collective-permute-start(f32[2,12,48,1,128]{4,2,3,1,0:T(8,128)S(1)} %copy.39), channel_id=1, source_target_pairs={{0,1},{1,2},{2,3},{3,4},{4,5},{5,6},{6,7},{7,8},{8,9},{9,10},{10,1... | collective-permute-start | bytes 1769480 | tf_op jit(solution)/shard_map/ppermute | solution.py:15
  151.0 64.5 %collective-permute-start.5 = (f32[2,12,48,1,128]{4,2,3,1,0:T(8,128)S(1)}, f32[2,12,48,1,128]{4,2,3,1,0:T(8,128)S(1)}, u32[]{:S(2)}, u32[]{:S(2)}) collective-permute-start(f32[2,12,48,1,128]{4,2,3,1,0:T(8,128)S(1)} %copy.46), channel_id=1, source_target_pairs={{1,0},{2,1},{3,2},{4,3},{5,4},{6,5},{7,6},{8,7},{9,8},{10,9},{11,1... | collective-permute-start | bytes 1769480 | tf_op jit(solution)/shard_map/ppermute | solution.py:18
  155.8 59.9 %collective-permute-start.4 = (f32[2,12,48,1,128]{4,2,3,1,0:T(8,128)S(1)}, f32[2,12,48,1,128]{4,2,3,1,0:T(8,128)S(1)}, u32[]{:S(2)}, u32[]{:S(2)}) collective-permute-start(f32[2,12,48,1,128]{4,2,3,1,0:T(8,128)S(1)} %copy.46), channel_id=1, source_target_pairs={{0,1},{1,2},{2,3},{3,4},{4,5},{5,6},{6,7},{7,8},{8,9},{9,10},{10,1... | collective-permute-start | bytes 1769480 | tf_op jit(solution)/shard_map/ppermute | solution.py:15
  220.8 145.4 %copy-start.2 = (f32[1,128]{1,0:T(1,128)S(1)}, f32[1,128]{1,0:T(1,128)}, u32[]{:S(2)}) copy-start(f32[1,128]{1,0:T(1,128)} %param.11) | copy-start | bytes 1540
  221.0 146.1 %collective-permute-start.7 = (f32[2,12,48,1,128]{4,2,3,1,0:T(8,128)S(1)}, f32[2,12,48,1,128]{4,2,3,1,0:T(8,128)S(1)}, u32[]{:S(2)}, u32[]{:S(2)}) collective-permute-start(f32[2,12,48,1,128]{4,2,3,1,0:T(8,128)S(1)} %copy.53), channel_id=1, source_target_pairs={{1,0},{2,1},{3,2},{4,3},{5,4},{6,5},{7,6},{8,7},{9,8},{10,9},{11,1... | collective-permute-start | bytes 1769480 | tf_op jit(solution)/shard_map/ppermute | solution.py:18
  226.3 141.0 %collective-permute-start.6 = (f32[2,12,48,1,128]{4,2,3,1,0:T(8,128)S(1)}, f32[2,12,48,1,128]{4,2,3,1,0:T(8,128)S(1)}, u32[]{:S(2)}, u32[]{:S(2)}) collective-permute-start(f32[2,12,48,1,128]{4,2,3,1,0:T(8,128)S(1)} %copy.53), channel_id=1, source_target_pairs={{0,1},{1,2},{2,3},{3,4},{4,5},{5,6},{6,7},{7,8},{8,9},{9,10},{10,1... | collective-permute-start | bytes 1769480 | tf_op jit(solution)/shard_map/ppermute | solution.py:15
  372.7 21.4 %collective-permute-start.9 = (f32[2,12,48,1,128]{4,2,3,1,0:T(8,128)S(1)}, f32[2,12,48,1,128]{4,2,3,1,0:T(8,128)S(1)}, u32[]{:S(2)}, u32[]{:S(2)}) collective-permute-start(f32[2,12,48,1,128]{4,2,3,1,0:T(8,128)S(1)} %copy.60), channel_id=1, source_target_pairs={{1,0},{2,1},{3,2},{4,3},{5,4},{6,5},{7,6},{8,7},{9,8},{10,9},{11,1... | collective-permute-start | bytes 1769480 | tf_op jit(solution)/shard_map/ppermute | solution.py:18
  380.4 26.5 %collective-permute-start.8 = (f32[2,12,48,1,128]{4,2,3,1,0:T(8,128)S(1)}, f32[2,12,48,1,128]{4,2,3,1,0:T(8,128)S(1)}, u32[]{:S(2)}, u32[]{:S(2)}) collective-permute-start(f32[2,12,48,1,128]{4,2,3,1,0:T(8,128)S(1)} %copy.60), channel_id=1, source_target_pairs={{0,1},{1,2},{2,3},{3,4},{4,5},{5,6},{6,7},{7,8},{8,9},{9,10},{10,1... | collective-permute-start | bytes 1769480 | tf_op jit(solution)/shard_map/ppermute | solution.py:15
  412.2 29.5 %collective-permute-start.11 = (f32[2,12,48,1,128]{4,2,3,1,0:T(8,128)S(1)}, f32[2,12,48,1,128]{4,2,3,1,0:T(8,128)S(1)}, u32[]{:S(2)}, u32[]{:S(2)}) collective-permute-start(f32[2,12,48,1,128]{4,2,3,1,0:T(8,128)S(1)} %copy.67), channel_id=1, source_target_pairs={{1,0},{2,1},{3,2},{4,3},{5,4},{6,5},{7,6},{8,7},{9,8},{10,9},{11,1... | collective-permute-start | bytes 1769480 | tf_op jit(solution)/shard_map/ppermute | solution.py:18
  417.8 25.8 %collective-permute-start.10 = (f32[2,12,48,1,128]{4,2,3,1,0:T(8,128)S(1)}, f32[2,12,48,1,128]{4,2,3,1,0:T(8,128)S(1)}, u32[]{:S(2)}, u32[]{:S(2)}) collective-permute-start(f32[2,12,48,1,128]{4,2,3,1,0:T(8,128)S(1)} %copy.67), channel_id=1, source_target_pairs={{0,1},{1,2},{2,3},{3,4},{4,5},{5,6},{6,7},{7,8},{8,9},{9,10},{10,1... | collective-permute-start | bytes 1769480 | tf_op jit(solution)/shard_map/ppermute | solution.py:15
where the time goes:
time: 680 us
  blocking collectives  535 us (79%)
  starting transfers between devices  54.6 us (8%)
  waiting for transfers between devices  43.7 us (6%)
  other arithmetic  26.3 us (4%)
  matrix products  9.1 us (1%)
  local copies, waits for them, and re-layouts  8.41 us (1%)
    all_gather x6, blocking collectives, per_device(): lax.all_gather(state, 'obj', axis=1, tiled=True)  307 us
    psum x1, blocking collectives, per_device(): partial_sum = lax.psum(partial_sum, 'tile')  228 us
    ppermute x6, starting transfers between devices, padded_2(): lax.ppermute(lax.slice_in_dim(block, 0, width, axis=dim), axis, backward)  42.3 us
    ppermute x6, waiting for transfers between devices, padded_2(): lax.ppermute(lax.slice_in_dim(block, 0, width, axis=dim), axis, backward)  29.4 us
    unnamed x144, other arithmetic  14.8 us
    ppermute x6, waiting for transfers between devices, padded_2(): lax.ppermute(lax.slice_in_dim(block, block.shape[dim] - width, None, axis...  14.3 us
  transfers between devices with their start and end apart: 12, of which 4 were waited for; matrix products, arithmetic and copies ran while one was open for 1% of the time, Pallas kernels for 0%

commit v1 on v0

--- a/solution.py
+++ b/solution.py
@@ -79,7 +79,12 @@
         partials[moment] = partial_sum
         state = checkpoints[moment]
         adjoint = react_back(
-            solved, lax.all_gather(state, "obj", axis=1, tiled=True), coupling, recombination
+            solved,
+            jnp.concatenate(
+                lax.all_to_all(jnp.stack([state] * lax.axis_size("obj")), "obj", 0, 0), axis=1
+            ),
+            coupling,
+            recombination,
         )
     gradients = jnp.stack(partials)
     return (adjoint[None], (gradients / cells)[None])

time: 680 us -> 628 us (0.924); the launches traced: 680 us -> 620 us
  blocking collectives: 535 us -> 225 us
  starting transfers between devices: 54.6 us -> 163 us
  other arithmetic: 26.3 us -> 131 us
  local copies, waits for them, and re-layouts: 8.41 us -> 24.5 us
  waiting for transfers between devices: 43.7 us -> 59.7 us
    all_gather x6 -> x0, blocking collectives: 307 us -> none  [per_device(): lax.all_gather(state, 'obj', axis=1, tiled=True)]
    all_to_all x0 -> x6, starting transfers between devices: none -> 102 us  [per_device(): lax.all_to_all(jnp.stack([state] * lax.axis_size('obj')), 'obj', 0, 0)]
    unnamed x144, other arithmetic: 14.8 us -> 103 us
    ppermute x6, waiting for transfers between devices: 14.3 us -> 28.3 us  [padded_2(): lax.ppermute(lax.slice_in_dim(block, block.shape[dim] - width, None, axis...]
    sub x10, other arithmetic: 4.03 us -> 13.9 us  [per_device(): lax.linalg.tridiagonal_solve(-below, middle, -above, advected.reshape(fie...]
  transfers between devices with their start and end apart: 12 -> 18, of which waited for: 4 -> 6; matrix products, arithmetic and copies ran while one was open for 1% -> 24% of each run, Pallas kernels for 0% -> 0%
where the time goes in v1:
time: 628 us; the launch traced here: 620 us
  blocking collectives  225 us (36%)
  starting transfers between devices  163 us (26%)
  other arithmetic  131 us (21%)
  waiting for transfers between devices  59.7 us (10%)
  local copies, waits for them, and re-layouts  24.5 us (4%)
  matrix products  12.6 us (2%)
    psum x1, blocking collectives, per_device(): partial_sum = lax.psum(partial_sum, 'tile')  225 us
    unnamed x144, other arithmetic  103 us
    all_to_all x6, starting transfers between devices, per_device(): lax.all_to_all(jnp.stack([state] * lax.axis_size('obj')), 'obj', 0, 0)  102 us
    ppermute x6, starting transfers between devices, padded_2(): lax.ppermute(lax.slice_in_dim(block, 0, width, axis=dim), axis, backward)  47.4 us
    ppermute x6, waiting for transfers between devices, padded_2(): lax.ppermute(lax.slice_in_dim(block, 0, width, axis=dim), axis, backward)  31.4 us
    ppermute x6, waiting for transfers between devices, padded_2(): lax.ppermute(lax.slice_in_dim(block, block.shape[dim] - width, None, axis...  28.3 us
    sub x10, other arithmetic, per_device(): lax.linalg.tridiagonal_solve(-below, middle, -above, advected.reshape(fie...  13.9 us
    ppermute x6, starting transfers between devices, padded_2(): lax.ppermute(lax.slice_in_dim(block, block.shape[dim] - width, None, axis...  13.5 us
  transfers between devices with their start and end apart: 18, of which 6 were waited for; matrix products, arithmetic and copies ran while one was open for 24% of the time, Pallas kernels for 0%

profile of v1, /device:TPU:2, one launch (start us, length us, event | category | flops | bytes accessed | tf_op | source)
XLA Modules:
  0.0 619.6 jit_solution(18361586602518207791)
XLA Ops:
  5.2 15.6 %collective-permute-start.1 = (f32[2,12,48,1,128]{4,2,3,1,0:T(8,128)S(1)}, f32[2,12,48,1,128]{4,2,3,1,0:T(8,128)S(1)}, u32[]{:S(2)}, u32[]{:S(2)}) collective-permute-start(f32[2,12,48,1,128]{4,2,3,1,0:T(8,128)S(1)} %copy.31), channel_id=1, source_target_pairs={{1,0},{2,1},{3,2},{4,3},{5,4},{6,5},{7,6},{8,7},{9,8},{10,9},{11,1... | collective-permute-start | bytes 1769480 | tf_op jit(solution)/shard_map/ppermute | solution.py:18
  20.8 1.9 collective-permute-start
  24.1 10.6 %all-to-all-start = ((bf16[16,12,3,1,128]{4,1,2,3,0:T(8,128)(2,1)}), bf16[16,12,3,1,128]{4,1,2,3,0:T(8,128)(2,1)S(1)}, u32[]{:S(2)}, u32[]{:S(2)}) async-start(bf16[16,12,3,1,128]{4,1,2,3,0:T(8,128)(2,1)} %stack.90), calls=%async_computation | async-start | bytes 393216 | tf_op jit(solution)/shard_map/all_to_all | solution.py:84
  42.0 10.8 %collective-permute-done = f32[2,12,48,1,128]{4,2,3,1,0:T(8,128)S(1)} collective-permute-done((f32[2,12,48,1,128]{4,2,3,1,0:T(8,128)S(1)}, f32[2,12,48,1,128]{4,2,3,1,0:T(8,128)S(1)}, u32[]{:S(2)}, u32[]{:S(2)}) %collective-permute-start) | collective-permute-done | bytes 589856 | tf_op jit(solution)/shard_map/ppermute | solution.py:15
  54.0 1.9 fusion.1132
  55.9 1.6 constant_dynamic-update-slice_fusion.46
  73.9 1.3 fusion.13
  75.5 5.7 collective-permute-start.3
  81.2 1.9 collective-permute-start.2
  83.9 11.2 %all-to-all-start.1 = ((bf16[16,12,3,1,128]{4,1,2,3,0:T(8,128)(2,1)}), bf16[16,12,3,1,128]{4,1,2,3,0:T(8,128)(2,1)S(1)}, u32[]{:S(2)}, u32[]{:S(2)}) async-start(bf16[16,12,3,1,128]{4,1,2,3,0:T(8,128)(2,1)} %stack.94), calls=%async_computation.1 | async-start | bytes 393216 | tf_op jit(solution)/shard_map/all_to_all | solution.py:84
  95.0 12.2 %collective-permute-done.3 = f32[2,12,48,1,128]{4,2,3,1,0:T(8,128)} collective-permute-done((f32[2,12,48,1,128]{4,2,3,1,0:T(8,128)S(1)}, f32[2,12,48,1,128]{4,2,3,1,0:T(8,128)}, u32[]{:S(2)}, u32[]{:S(2)}) %collective-permute-start.3) | collective-permute-done | bytes 589856 | tf_op jit(solution)/shard_map/ppermute | solution.py:18
  107.2 1.3 copy.43
  109.7 1.9 fusion.953
  111.6 1.6 constant_dynamic-update-slice_fusion.93
  129.6 1.3 fusion.14
  131.1 8.1 %collective-permute-start.5 = (f32[2,12,48,1,128]{4,2,3,1,0:T(8,128)S(1)}, f32[2,12,48,1,128]{4,2,3,1,0:T(8,128)}, u32[]{:S(2)}, u32[]{:S(2)}) collective-permute-start(f32[2,12,48,1,128]{4,2,3,1,0:T(8,128)S(1)} %copy.46), channel_id=1, source_target_pairs={{1,0},{2,1},{3,2},{4,3},{5,4},{6,5},{7,6},{8,7},{9,8},{10,9},{11,1... | collective-permute-start | bytes 1769480 | tf_op jit(solution)/shard_map/ppermute | solution.py:18
  139.3 1.9 collective-permute-start.4
  141.9 12.3 %all-to-all-start.2 = ((bf16[16,12,3,1,128]{4,1,2,3,0:T(8,128)(2,1)}), bf16[16,12,3,1,128]{4,1,2,3,0:T(8,128)(2,1)S(1)}, u32[]{:S(2)}, u32[]{:S(2)}) async-start(bf16[16,12,3,1,128]{4,1,2,3,0:T(8,128)(2,1)} %stack.98), calls=%async_computation.2 | async-start | bytes 393216 | tf_op jit(solution)/shard_map/all_to_all | solution.py:84
  154.2 8.2 %collective-permute-done.5 = f32[2,12,48,1,128]{4,2,3,1,0:T(8,128)} collective-permute-done((f32[2,12,48,1,128]{4,2,3,1,0:T(8,128)S(1)}, f32[2,12,48,1,128]{4,2,3,1,0:T(8,128)}, u32[]{:S(2)}, u32[]{:S(2)}) %collective-permute-start.5) | collective-permute-done | bytes 589856 | tf_op jit(solution)/shard_map/ppermute | solution.py:18
  162.4 1.3 copy.49
  163.7 1.3 copy.48
  166.0 1.9 fusion.780
  167.9 1.6 constant_dynamic-update-slice_fusion.140
  188.3 7.2 %collective-permute-start.7 = (f32[2,12,48,1,128]{4,2,3,1,0:T(8,128)}, f32[2,12,48,1,128]{4,2,3,1,0:T(8,128)}, u32[]{:S(2)}, u32[]{:S(2)}) collective-permute-start(f32[2,12,48,1,128]{4,2,3,1,0:T(8,128)} %copy.52), channel_id=1, source_target_pairs={{1,0},{2,1},{3,2},{4,3},{5,4},{6,5},{7,6},{8,7},{9,8},{10,9},{11,1... | collective-permute-start | bytes 1769480 | tf_op jit(solution)/shard_map/ppermute | solution.py:18
  195.5 1.9 collective-permute-start.6
  198.2 18.0 %all-to-all-start.3 = ((bf16[16,12,3,1,128]{4,1,2,3,0:T(8,128)(2,1)}), bf16[16,12,3,1,128]{4,1,2,3,0:T(8,128)(2,1)S(1)}, u32[]{:S(2)}, u32[]{:S(2)}) async-start(bf16[16,12,3,1,128]{4,1,2,3,0:T(8,128)(2,1)} %stack.102), calls=%async_computation.3 | async-start | bytes 393216 | tf_op jit(solution)/shard_map/all_to_all | solution.py:84
  216.2 1.3 copy.55
  217.5 1.3 copy.54
  219.8 1.9 fusion.607
  221.7 1.6 constant_dynamic-update-slice_fusion.187
  238.0 1.3 constant_dynamic-update-slice_fusion.145
  240.2 1.3 fusion.16
  242.7 8.8 %collective-permute-start.9 = (f32[2,12,48,1,128]{4,2,3,1,0:T(8,128)}, f32[2,12,48,1,128]{4,2,3,1,0:T(8,128)}, u32[]{:S(2)}, u32[]{:S(2)}) collective-permute-start(f32[2,12,48,1,128]{4,2,3,1,0:T(8,128)} %copy.58), channel_id=1, source_target_pairs={{1,0},{2,1},{3,2},{4,3},{5,4},{6,5},{7,6},{8,7},{9,8},{10,9},{11,1... | collective-permute-start | bytes 1769480 | tf_op jit(solution)/shard_map/ppermute | solution.py:18
  251.5 1.9 collective-permute-start.8
  254.1 19.7 %all-to-all-start.4 = ((bf16[16,12,3,1,128]{4,1,2,3,0:T(8,128)(2,1)}), bf16[16,12,3,1,128]{4,1,2,3,0:T(8,128)(2,1)S(1)}, u32[]{:S(2)}, u32[]{:S(2)}) async-start(bf16[16,12,3,1,128]{4,1,2,3,0:T(8,128)(2,1)} %stack.106), calls=%async_computation.4 | async-start | bytes 393216 | tf_op jit(solution)/shard_map/all_to_all | solution.py:84
  275.9 1.3 copy.61
  278.3 1.3 copy.60
  281.3 1.9 fusion.434
  283.2 1.6 constant_dynamic-update-slice_fusion.234
  301.2 30.4 %all-to-all-start.5 = ((bf16[16,12,3,1,128]{4,1,2,3,0:T(8,128)(2,1)}), bf16[16,12,3,1,128]{4,1,2,3,0:T(8,128)(2,1)S(1)}, u32[]{:S(2)}, u32[]{:S(2)}) async-start(bf16[16,12,3,1,128]{4,1,2,3,0:T(8,128)(2,1)} %stack.110), calls=%async_computation.5 | async-start | bytes 393216 | tf_op jit(solution)/shard_map/all_to_all | solution.py:84
  332.3 1.3 fusion.17
  333.9 1.9 collective-permute-start.11
  335.8 3.9 collective-permute-start.10
  342.7 11.0 %collective-permute-done.11 = f32[2,12,48,1,128]{4,2,3,1,0:T(8,128)S(1)} collective-permute-done((f32[2,12,48,1,128]{4,2,3,1,0:T(8,128)S(1)}, f32[2,12,48,1,128]{4,2,3,1,0:T(8,128)S(1)}, u32[]{:S(2)}, u32[]{:S(2)}) %collective-permute-start.11) | collective-permute-done | bytes 589856 | tf_op jit(solution)/shard_map/ppermute | solution.py:18
  353.9 16.4 %collective-permute-done.10 = f32[2,12,48,1,128]{4,2,3,1,0:T(8,128)S(1)} collective-permute-done((f32[2,12,48,1,128]{4,2,3,1,0:T(8,128)S(1)}, f32[2,12,48,1,128]{4,2,3,1,0:T(8,128)S(1)}, u32[]{:S(2)}, u32[]{:S(2)}) %collective-permute-start.10) | collective-permute-done | bytes 589856 | tf_op jit(solution)/shard_map/ppermute | solution.py:15
  371.6 1.9 fusion.261
  373.5 1.6 constant_dynamic-update-slice_fusion.281
  394.0 224.7 %all-reduce.14 = (f32[1,1,12,48]{3,0,2,1:T(1,128)S(1)}, f32[1,1,12,48]{3,0,2,1:T(1,128)S(1)}, f32[1,1,12,48]{3,0,2,1:T(1,128)S(1)}, f32[1,1,12,48]{3,0,2,1:T(1,1...) all-reduce(f32[1,1,12,48]{3,0,2,1:T(1,128)S(1)} %stack.111, ...), channel_id=1, replica_groups=mesh['obj'=16,'tile'=32] {'tile'}, use_global_device_ids=true, to_apply=%region_0.1 | all-reduce | flops 3456 | bytes 27648 | tf_op jit(solution)/shard_map/psum | solution.py:78
  (572 shorter events, 133.5 us)
Async XLA Ops:
  5.2 36.6 %collective-permute-start.1 = (f32[2,12,48,1,128]{4,2,3,1,0:T(8,128)S(1)}, f32[2,12,48,1,128]{4,2,3,1,0:T(8,128)S(1)}, u32[]{:S(2)}, u32[]{:S(2)}) collective-permute-start(f32[2,12,48,1,128]{4,2,3,1,0:T(8,128)S(1)} %copy.31), channel_id=1, source_target_pairs={{1,0},{2,1},{3,2},{4,3},{5,4},{6,5},{7,6},{8,7},{9,8},{10,9},{11,1... | collective-permute-start | bytes 1769480 | tf_op jit(solution)/shard_map/ppermute | solution.py:18
  20.8 32.0 %collective-permute-start = (f32[2,12,48,1,128]{4,2,3,1,0:T(8,128)S(1)}, f32[2,12,48,1,128]{4,2,3,1,0:T(8,128)S(1)}, u32[]{:S(2)}, u32[]{:S(2)}) collective-permute-start(f32[2,12,48,1,128]{4,2,3,1,0:T(8,128)S(1)} %copy.31), channel_id=1, source_target_pairs={{0,1},{1,2},{2,3},{3,4},{4,5},{5,6},{6,7},{7,8},{8,9},{9,10},{10,1... | collective-permute-start | bytes 1769480 | tf_op jit(solution)/shard_map/ppermute | solution.py:15
  24.1 49.0 %all-to-all-start = ((bf16[16,12,3,1,128]{4,1,2,3,0:T(8,128)(2,1)}), bf16[16,12,3,1,128]{4,1,2,3,0:T(8,128)(2,1)S(1)}, u32[]{:S(2)}, u32[]{:S(2)}) async-start(bf16[16,12,3,1,128]{4,1,2,3,0:T(8,128)(2,1)} %stack.90), calls=%async_computation | async-start | bytes 393216 | tf_op jit(solution)/shard_map/all_to_all | solution.py:84
  36.1 201.5 %copy-start.65 = (f32[12]{0:T(128)}, f32[12]{0:T(128)S(1)}, u32[]{:S(2)}) copy-start(f32[12]{0:T(128)S(1)} %get-tuple-element.698) | copy-start | bytes 148
  36.1 201.5 %copy-start.67 = (f32[12]{0:T(128)}, f32[12]{0:T(128)S(1)}, u32[]{:S(2)}) copy-start(f32[12]{0:T(128)S(1)} %get-tuple-element.699) | copy-start | bytes 148
  36.1 201.5 %copy-start.69 = (f32[12]{0:T(128)}, f32[12]{0:T(128)S(1)}, u32[]{:S(2)}) copy-start(f32[12]{0:T(128)S(1)} %get-tuple-element.700) | copy-start | bytes 148
  36.1 201.5 %copy-start.71 = (f32[12]{0:T(128)}, f32[12]{0:T(128)S(1)}, u32[]{:S(2)}) copy-start(f32[12]{0:T(128)S(1)} %get-tuple-element.701) | copy-start | bytes 148
  36.1 201.5 %copy-start.73 = (f32[12]{0:T(128)}, f32[12]{0:T(128)S(1)}, u32[]{:S(2)}) copy-start(f32[12]{0:T(128)S(1)} %get-tuple-element.702) | copy-start | bytes 148
  36.1 201.5 %copy-start.75 = (f32[12]{0:T(128)}, f32[12]{0:T(128)S(1)}, u32[]{:S(2)}) copy-start(f32[12]{0:T(128)S(1)} %get-tuple-element.703) | copy-start | bytes 148
  36.1 201.5 %copy-start.77 = (f32[12]{0:T(128)}, f32[12]{0:T(128)S(1)}, u32[]{:S(2)}) copy-start(f32[12]{0:T(128)S(1)} %get-tuple-element.704) | copy-start | bytes 148
  36.8 200.9 %copy-start.1 = (f32[12]{0:T(128)}, f32[12]{0:T(128)S(1)}, u32[]{:S(2)}) copy-start(f32[12]{0:T(128)S(1)} %get-tuple-element.715) | copy-start | bytes 148
  36.8 200.9 %copy-start.3 = (f32[12]{0:T(128)}, f32[12]{0:T(128)S(1)}, u32[]{:S(2)}) copy-start(f32[12]{0:T(128)S(1)} %get-tuple-element.730) | copy-start | bytes 148
  36.8 200.9 %copy-start.5 = (f32[12]{0:T(128)}, f32[12]{0:T(128)S(1)}, u32[]{:S(2)}) copy-start(f32[12]{0:T(128)S(1)} %get-tuple-element.732) | copy-start | bytes 148
  38.1 199.6 %copy-start.7 = (f32[12]{0:T(128)}, f32[12]{0:T(128)S(1)}, u32[]{:S(2)}) copy-start(f32[12]{0:T(128)S(1)} %get-tuple-element.639) | copy-start | bytes 148
  40.2 197.5 %copy-start.9 = (f32[12]{0:T(128)}, f32[12]{0:T(128)S(1)}, u32[]{:S(2)}) copy-start(f32[12]{0:T(128)S(1)} %get-tuple-element.556) | copy-start | bytes 148
  40.2 197.5 %copy-start.11 = (f32[12,1]{0,1:T(1,128)}, f32[12,1]{0,1:T(1,128)S(1)}, u32[]{:S(2)}) copy-start(f32[12,1]{0,1:T(1,128)S(1)} %get-tuple-element.558) | copy-start | bytes 148
  40.2 197.5 %copy-start.13 = (f32[12,1]{0,1:T(1,128)}, f32[12,1]{0,1:T(1,128)S(1)}, u32[]{:S(2)}) copy-start(f32[12,1]{0,1:T(1,128)S(1)} %get-tuple-element.560) | copy-start | bytes 148
  40.2 197.5 %copy-start.15 = (f32[12,1]{0,1:T(1,128)}, f32[12,1]{0,1:T(1,128)S(1)}, u32[]{:S(2)}) copy-start(f32[12,1]{0,1:T(1,128)S(1)} %get-tuple-element.562) | copy-start | bytes 148
  40.2 197.5 %copy-start.17 = (f32[12,1]{0,1:T(1,128)}, f32[12,1]{0,1:T(1,128)S(1)}, u32[]{:S(2)}) copy-start(f32[12,1]{0,1:T(1,128)S(1)} %get-tuple-element.564) | copy-start | bytes 148
  40.2 197.5 %copy-start.19 = (f32[12,1]{0,1:T(1,128)}, f32[12,1]{0,1:T(1,128)S(1)}, u32[]{:S(2)}) copy-start(f32[12,1]{0,1:T(1,128)S(1)} %get-tuple-element.566) | copy-start | bytes 148
  40.2 197.5 %copy-start.21 = (f32[12,1]{0,1:T(1,128)}, f32[12,1]{0,1:T(1,128)S(1)}, u32[]{:S(2)}) copy-start(f32[12,1]{0,1:T(1,128)S(1)} %get-tuple-element.568) | copy-start | bytes 148
  40.2 197.5 %copy-start.23 = (f32[12,1]{0,1:T(1,128)}, f32[12,1]{0,1:T(1,128)S(1)}, u32[]{:S(2)}) copy-start(f32[12,1]{0,1:T(1,128)S(1)} %get-tuple-element.570) | copy-start | bytes 148
  40.2 197.5 %copy-start.25 = (f32[12,1]{0,1:T(1,128)}, f32[12,1]{0,1:T(1,128)S(1)}, u32[]{:S(2)}) copy-start(f32[12,1]{0,1:T(1,128)S(1)} %get-tuple-element.572) | copy-start | bytes 148
  40.3 197.5 %copy-start.27 = (f32[12,1]{0,1:T(1,128)}, f32[12,1]{0,1:T(1,128)S(1)}, u32[]{:S(2)}) copy-start(f32[12,1]{0,1:T(1,128)S(1)} %get-tuple-element.574) | copy-start | bytes 148
  40.3 197.5 %copy-start.29 = (f32[12,1]{0,1:T(1,128)}, f32[12,1]{0,1:T(1,128)S(1)}, u32[]{:S(2)}) copy-start(f32[12,1]{0,1:T(1,128)S(1)} %get-tuple-element.576) | copy-start | bytes 148
  40.3 197.5 %copy-start.31 = (f32[12,1]{0,1:T(1,128)}, f32[12,1]{0,1:T(1,128)S(1)}, u32[]{:S(2)}) copy-start(f32[12,1]{0,1:T(1,128)S(1)} %get-tuple-element.578) | copy-start | bytes 148
  40.3 197.5 %copy-start.33 = (f32[12,1]{0,1:T(1,128)}, f32[12,1]{0,1:T(1,128)S(1)}, u32[]{:S(2)}) copy-start(f32[12,1]{0,1:T(1,128)S(1)} %get-tuple-element.580) | copy-start | bytes 148
  40.3 197.5 %copy-start.35 = (f32[12,1]{0,1:T(1,128)}, f32[12,1]{0,1:T(1,128)S(1)}, u32[]{:S(2)}) copy-start(f32[12,1]{0,1:T(1,128)S(1)} %get-tuple-element.582) | copy-start | bytes 148
  40.3 197.5 %copy-start.37 = (f32[12,1]{0,1:T(1,128)}, f32[12,1]{0,1:T(1,128)S(1)}, u32[]{:S(2)}) copy-start(f32[12,1]{0,1:T(1,128)S(1)} %get-tuple-element.584) | copy-start | bytes 148
  40.3 197.5 %copy-start.39 = (f32[12,1]{0,1:T(1,128)}, f32[12,1]{0,1:T(1,128)S(1)}, u32[]{:S(2)}) copy-start(f32[12,1]{0,1:T(1,128)S(1)} %get-tuple-element.586) | copy-start | bytes 148
  40.3 197.5 %copy-start.41 = (f32[12,1]{0,1:T(1,128)}, f32[12,1]{0,1:T(1,128)S(1)}, u32[]{:S(2)}) copy-start(f32[12,1]{0,1:T(1,128)S(1)} %get-tuple-element.588) | copy-start | bytes 148
  40.3 197.5 %copy-start.43 = (f32[12,1]{0,1:T(1,128)}, f32[12,1]{0,1:T(1,128)S(1)}, u32[]{:S(2)}) copy-start(f32[12,1]{0,1:T(1,128)S(1)} %get-tuple-element.590) | copy-start | bytes 148
  40.3 197.5 %copy-start.45 = (f32[12,1]{0,1:T(1,128)}, f32[12,1]{0,1:T(1,128)S(1)}, u32[]{:S(2)}) copy-start(f32[12,1]{0,1:T(1,128)S(1)} %get-tuple-element.592) | copy-start | bytes 148
  75.5 31.7 %collective-permute-start.3 = (f32[2,12,48,1,128]{4,2,3,1,0:T(8,128)S(1)}, f32[2,12,48,1,128]{4,2,3,1,0:T(8,128)}, u32[]{:S(2)}, u32[]{:S(2)}) collective-permute-start(f32[2,12,48,1,128]{4,2,3,1,0:T(8,128)S(1)} %copy.40), channel_id=1, source_target_pairs={{1,0},{2,1},{3,2},{4,3},{5,4},{6,5},{7,6},{8,7},{9,8},{10,9},{11,1... | collective-permute-start | bytes 1769480 | tf_op jit(solution)/shard_map/ppermute | solution.py:18
  81.2 27.2 %collective-permute-start.2 = (f32[2,12,48,1,128]{4,2,3,1,0:T(8,128)S(1)}, f32[2,12,48,1,128]{4,2,3,1,0:T(8,128)S(1)}, u32[]{:S(2)}, u32[]{:S(2)}) collective-permute-start(f32[2,12,48,1,128]{4,2,3,1,0:T(8,128)S(1)} %copy.40), channel_id=1, source_target_pairs={{0,1},{1,2},{2,3},{3,4},{4,5},{5,6},{6,7},{7,8},{8,9},{9,10},{10,1... | collective-permute-start | bytes 1769480 | tf_op jit(solution)/shard_map/ppermute | solution.py:15
  83.9 45.0 %all-to-all-start.1 = ((bf16[16,12,3,1,128]{4,1,2,3,0:T(8,128)(2,1)}), bf16[16,12,3,1,128]{4,1,2,3,0:T(8,128)(2,1)S(1)}, u32[]{:S(2)}, u32[]{:S(2)}) async-start(bf16[16,12,3,1,128]{4,1,2,3,0:T(8,128)(2,1)} %stack.94), calls=%async_computation.1 | async-start | bytes 393216 | tf_op jit(solution)/shard_map/all_to_all | solution.py:84
  131.1 31.3 %collective-permute-start.5 = (f32[2,12,48,1,128]{4,2,3,1,0:T(8,128)S(1)}, f32[2,12,48,1,128]{4,2,3,1,0:T(8,128)}, u32[]{:S(2)}, u32[]{:S(2)}) collective-permute-start(f32[2,12,48,1,128]{4,2,3,1,0:T(8,128)S(1)} %copy.46), channel_id=1, source_target_pairs={{1,0},{2,1},{3,2},{4,3},{5,4},{6,5},{7,6},{8,7},{9,8},{10,9},{11,1... | collective-permute-start | bytes 1769480 | tf_op jit(solution)/shard_map/ppermute | solution.py:18
  139.3 24.4 %collective-permute-start.4 = (f32[2,12,48,1,128]{4,2,3,1,0:T(8,128)S(1)}, f32[2,12,48,1,128]{4,2,3,1,0:T(8,128)}, u32[]{:S(2)}, u32[]{:S(2)}) collective-permute-start(f32[2,12,48,1,128]{4,2,3,1,0:T(8,128)S(1)} %copy.46), channel_id=1, source_target_pairs={{0,1},{1,2},{2,3},{3,4},{4,5},{5,6},{6,7},{7,8},{8,9},{9,10},{10,1... | collective-permute-start | bytes 1769480 | tf_op jit(solution)/shard_map/ppermute | solution.py:15
  141.9 43.2 %all-to-all-start.2 = ((bf16[16,12,3,1,128]{4,1,2,3,0:T(8,128)(2,1)}), bf16[16,12,3,1,128]{4,1,2,3,0:T(8,128)(2,1)S(1)}, u32[]{:S(2)}, u32[]{:S(2)}) async-start(bf16[16,12,3,1,128]{4,1,2,3,0:T(8,128)(2,1)} %stack.98), calls=%async_computation.2 | async-start | bytes 393216 | tf_op jit(solution)/shard_map/all_to_all | solution.py:84
  188.3 27.9 %collective-permute-start.7 = (f32[2,12,48,1,128]{4,2,3,1,0:T(8,128)}, f32[2,12,48,1,128]{4,2,3,1,0:T(8,128)}, u32[]{:S(2)}, u32[]{:S(2)}) collective-permute-start(f32[2,12,48,1,128]{4,2,3,1,0:T(8,128)} %copy.52), channel_id=1, source_target_pairs={{1,0},{2,1},{3,2},{4,3},{5,4},{6,5},{7,6},{8,7},{9,8},{10,9},{11,1... | collective-permute-start | bytes 1769480 | tf_op jit(solution)/shard_map/ppermute | solution.py:18
  195.5 21.9 %collective-permute-start.6 = (f32[2,12,48,1,128]{4,2,3,1,0:T(8,128)}, f32[2,12,48,1,128]{4,2,3,1,0:T(8,128)}, u32[]{:S(2)}, u32[]{:S(2)}) collective-permute-start(f32[2,12,48,1,128]{4,2,3,1,0:T(8,128)} %copy.52), channel_id=1, source_target_pairs={{0,1},{1,2},{2,3},{3,4},{4,5},{5,6},{6,7},{7,8},{8,9},{9,10},{10,1... | collective-permute-start | bytes 1769480 | tf_op jit(solution)/shard_map/ppermute | solution.py:15
  198.2 41.3 %all-to-all-start.3 = ((bf16[16,12,3,1,128]{4,1,2,3,0:T(8,128)(2,1)}), bf16[16,12,3,1,128]{4,1,2,3,0:T(8,128)(2,1)S(1)}, u32[]{:S(2)}, u32[]{:S(2)}) async-start(bf16[16,12,3,1,128]{4,1,2,3,0:T(8,128)(2,1)} %stack.102), calls=%async_computation.3 | async-start | bytes 393216 | tf_op jit(solution)/shard_map/all_to_all | solution.py:84
  242.7 33.2 %collective-permute-start.9 = (f32[2,12,48,1,128]{4,2,3,1,0:T(8,128)}, f32[2,12,48,1,128]{4,2,3,1,0:T(8,128)}, u32[]{:S(2)}, u32[]{:S(2)}) collective-permute-start(f32[2,12,48,1,128]{4,2,3,1,0:T(8,128)} %copy.58), channel_id=1, source_target_pairs={{1,0},{2,1},{3,2},{4,3},{5,4},{6,5},{7,6},{8,7},{9,8},{10,9},{11,1... | collective-permute-start | bytes 1769480 | tf_op jit(solution)/shard_map/ppermute | solution.py:18
  251.5 26.8 %collective-permute-start.8 = (f32[2,12,48,1,128]{4,2,3,1,0:T(8,128)}, f32[2,12,48,1,128]{4,2,3,1,0:T(8,128)}, u32[]{:S(2)}, u32[]{:S(2)}) collective-permute-start(f32[2,12,48,1,128]{4,2,3,1,0:T(8,128)} %copy.58), channel_id=1, source_target_pairs={{0,1},{1,2},{2,3},{3,4},{4,5},{5,6},{6,7},{7,8},{8,9},{9,10},{10,1... | collective-permute-start | bytes 1769480 | tf_op jit(solution)/shard_map/ppermute | solution.py:15
  254.1 46.3 %all-to-all-start.4 = ((bf16[16,12,3,1,128]{4,1,2,3,0:T(8,128)(2,1)}), bf16[16,12,3,1,128]{4,1,2,3,0:T(8,128)(2,1)S(1)}, u32[]{:S(2)}, u32[]{:S(2)}) async-start(bf16[16,12,3,1,128]{4,1,2,3,0:T(8,128)(2,1)} %stack.106), calls=%async_computation.4 | async-start | bytes 393216 | tf_op jit(solution)/shard_map/all_to_all | solution.py:84
  301.2 89.5 %all-to-all-start.5 = ((bf16[16,12,3,1,128]{4,1,2,3,0:T(8,128)(2,1)}), bf16[16,12,3,1,128]{4,1,2,3,0:T(8,128)(2,1)S(1)}, u32[]{:S(2)}, u32[]{:S(2)}) async-start(bf16[16,12,3,1,128]{4,1,2,3,0:T(8,128)(2,1)} %stack.110), calls=%async_computation.5 | async-start | bytes 393216 | tf_op jit(solution)/shard_map/all_to_all | solution.py:84
  333.9 19.8 %collective-permute-start.11 = (f32[2,12,48,1,128]{4,2,3,1,0:T(8,128)S(1)}, f32[2,12,48,1,128]{4,2,3,1,0:T(8,128)S(1)}, u32[]{:S(2)}, u32[]{:S(2)}) collective-permute-start(f32[2,12,48,1,128]{4,2,3,1,0:T(8,128)S(1)} %copy.64), channel_id=1, source_target_pairs={{1,0},{2,1},{3,2},{4,3},{5,4},{6,5},{7,6},{8,7},{9,8},{10,9},{11,1... | collective-permute-start | bytes 1769480 | tf_op jit(solution)/shard_map/ppermute | solution.py:18
  335.8 34.5 %collective-permute-start.10 = (f32[2,12,48,1,128]{4,2,3,1,0:T(8,128)S(1)}, f32[2,12,48,1,128]{4,2,3,1,0:T(8,128)S(1)}, u32[]{:S(2)}, u32[]{:S(2)}) collective-permute-start(f32[2,12,48,1,128]{4,2,3,1,0:T(8,128)S(1)} %copy.64), channel_id=1, source_target_pairs={{0,1},{1,2},{2,3},{3,4},{4,5},{5,6},{6,7},{7,8},{8,9},{9,10},{10,1... | collective-permute-start | bytes 1769480 | tf_op jit(solution)/shard_map/ppermute | solution.py:15
  (56 other events, 2066.1 us)
